TPU v7x, 128 devices: a whole 4x4x4 slice. The times are simulated.
128 devices in a mesh: ctx: 16 (over z, y), ch: 8 (over x, core).
Axes of the slice: x: 4, y: 4, z: 4, core: 2. Of those that a mesh axis runs over, the one named last changes fastest.
Arguments:
- outer_gate: bfloat16 [4096, 4096], P('ctx', 'ch'), may hold values from -6 to 6
- inner_gate: bfloat16 [4096, 4096], P('ctx', 'ch'), may hold values from -6 to 6
- values_in: bfloat16 [4096, 4096], P('ctx', 'ch'), may hold values from -6 to 6
- filters: float32 [4096, 4096], P('ctx', 'ch'), as said below
- skip_gain: float32 [4096], P('ch'), may hold values from 0.5 to 1.5
- w_out: bfloat16 [4096, 4096], P('ch', 'ctx'), may hold values from -0.125 to 0.125
Outputs:
- mixed: bfloat16 [4096, 4096], P('ctx', 'ch')
Inputs may be any that keep to these rules, and one draw needn't show every extreme that they name: `filters`: finite values.
All inputs are finite; a program needn't handle non-finite values.
Results may differ from a plain program's by a relative error of at most 0.022.
Values may be sent and summed in bfloat16 or wider, within the bound.
A program may use at most 64 MiB of HBM per device.

v0:
```python
import math
import jax
import jax.numpy as jnp
from jax import lax
from jax.sharding import PartitionSpec as P


def from_behind(block, axis, distance):
    devices = range(lax.axis_size(axis))
    route = [(i - distance, i) for i in devices if i - distance in devices]
    return lax.ppermute(block, axis, route)


def forward_table(block):
    length = 2 * block
    rows = jnp.arange(block, dtype=jnp.int32)[:, None]
    freqs = jnp.arange(length, dtype=jnp.int32)[None, :]
    angles = 2.0 * math.pi / length * (rows * freqs % length).astype(jnp.float32)
    return jnp.concatenate([jnp.cos(angles), -jnp.sin(angles)], axis=1)


def inverse_table(block):
    length = 2 * block
    freqs = jnp.arange(length, dtype=jnp.int32)[:, None]
    places = jnp.arange(length, dtype=jnp.int32)[None, :]
    angles = 2.0 * math.pi / length * (freqs * places % length).astype(jnp.float32)
    return jnp.concatenate([jnp.cos(angles), -jnp.sin(angles)], axis=0) / length


def split_table(table):
    upper_part = table.astype(jnp.bfloat16)
    lower_part = (table - upper_part.astype(jnp.float32)).astype(jnp.bfloat16)
    return (upper_part, lower_part)


def spectrum(series, table):
    return lax.dot_general(
        series,
        table,
        (((0,), (0,)), ((), ())),
        precision=lax.Precision.HIGH,
        preferred_element_type=jnp.float32,
    )


def narrow_spectrum(series, tables):
    dims = (((0,), (0,)), ((), ()))
    first = lax.dot_general(series, tables[0], dims, preferred_element_type=jnp.float32)
    return first + lax.dot_general(series, tables[1], dims, preferred_element_type=jnp.float32)


def complex_product(left, right):
    half = left.shape[-1] // 2
    left_re, left_im = (left[..., :half], left[..., half:])
    right_re, right_im = (right[..., :half], right[..., half:])
    return jnp.concatenate(
        [left_re * right_re - left_im * right_im, left_re * right_im + left_im * right_re], axis=-1
    )


def per_device(outer_gate, inner_gate, values_in, filters, skip_gain, w_out):
    block = outer_gate.shape[0]
    chans = outer_gate.shape[1]
    length = 2 * block
    gated = (inner_gate.astype(jnp.float32) * values_in.astype(jnp.float32)).astype(jnp.bfloat16)
    forward = forward_table(block)
    forward_parts = split_table(forward)
    inverse = inverse_table(block)
    whole_filter = lax.all_gather(filters.astype(jnp.bfloat16), "ctx", axis=0, tiled=True).astype(
        filters.dtype
    )
    mine = lax.axis_index("ctx")
    empty = jnp.zeros((chans, 2 * length), jnp.float32)
    piece = lax.all_gather(gated[None], "ctx", axis=0, tiled=True)

    def one_block(k, acc):
        distance = mine - k

        def live(inner):
            lag_rows = lax.dynamic_slice_in_dim(
                whole_filter, jnp.maximum(distance, 0) * block, block, 0
            )
            source = lax.dynamic_index_in_dim(piece, k, 0, keepdims=False)
            return inner + complex_product(
                narrow_spectrum(source, forward_parts), spectrum(lag_rows, forward)
            )

        return lax.cond(distance >= 0, live, lambda inner: inner, acc)

    summed = lax.fori_loop(0, piece.shape[0], one_block, empty)
    wave = lax.dot_general(
        inverse,
        summed,
        (((0,), (1,)), ((), ())),
        precision=lax.Precision.HIGH,
        preferred_element_type=jnp.float32,
    )
    carried = from_behind(wave[block:].astype(jnp.bfloat16), "ctx", 1).astype(jnp.float32)
    conv = wave[:block] + carried
    mix_in = (
        outer_gate.astype(jnp.float32) * (conv + skip_gain[None, :] * gated.astype(jnp.float32))
    ).astype(jnp.bfloat16)
    partial_rows = jnp.dot(
        mix_in, lax.all_gather(w_out, "ctx", axis=1, tiled=True), preferred_element_type=jnp.float32
    )
    return lax.psum_scatter(
        partial_rows.astype(jnp.bfloat16), "ch", scatter_dimension=1, tiled=True
    )


def solution(mesh):
    placed = (
        P("ctx", "ch"),
        P("ctx", "ch"),
        P("ctx", "ch"),
        P("ctx", "ch"),
        P("ch"),
        P("ch", "ctx"),
    )
    return jax.shard_map(
        per_device, mesh=mesh, in_specs=placed, out_specs=P("ctx", "ch"), check_vma=False
    )
```

profile of v0, /device:TPU:0, one launch (start us, length us, event | category | flops | bytes accessed | tf_op | source)
XLA Modules:
  0.0 322.4 jit_solution(1819847222807152443)
XLA Ops:
  6.5 0.0 all-gather.5.cloned.1.call-start
  6.5 1.8 convert_element_type.66
  8.3 0.0 all-gather.5.cloned.1.call-update
  8.3 0.0 all-gather.9.cloned.1.call-start
  8.4 1.8 multiply_convert_fusion
  10.2 0.0 all-gather.9.cloned.1.call-update
  10.2 0.0 all-gather.7.cloned.1.call-start
  10.3 0.7 all-gather.7.cloned.1.call-update
  10.9 0.0 reduce-scatter.2.cloned.1.call-start
  11.0 2.1 sine_negate_fusion.1
  13.1 0.9 fusion.35
  13.9 1.0 pad_maximum_fusion
  14.9 5.0 %sine_negate_fusion = (f32[512,512]{1,0:T(8,128)}, f32[512,512]{1,0:T(8,128)}) fusion(), kind=kLoop, calls=%fused_computation.28 | loop fusion | flops 3932160 | bytes 2097152 | tf_op jit(solution)/shard_map/neg | solution.py:27
  19.9 43.8 %all-gather.5.cloned.1.call-done = bf16[4096,512]{1,0:T(8,128)(2,1)} async-done(((bf16[256,512]{1,0:T(8,128)(2,1)}), bf16[4096,512]{1,0:T(8,128)(2,1)}) %all-gather.5.cloned.1.call-update) | async-done | bytes 4194320 | tf_op jit(solution)/shard_map/all_gather | solution.py:69
  63.7 6.6 %convert_element_type.67 = f32[4096,512]{1,0:T(8,128)} convert(bf16[4096,512]{1,0:T(8,128)(2,1)} %all-gather.5.cloned.1.call-done) | non-fusion elementwise | flops 2097152 | bytes 12582912 | tf_op jit(solution)/shard_map/convert_element_type | solution.py:69
  70.3 46.8 %all-gather.9.cloned.1.call-done = bf16[4096,512]{1,0:T(8,128)(2,1)} async-done(((bf16[256,512]{1,0:T(8,128)(2,1)}), bf16[4096,512]{1,0:T(8,128)(2,1)}) %all-gather.9.cloned.1.call-update) | async-done | bytes 4194320 | tf_op jit(solution)/shard_map/all_gather | solution.py:74
  117.1 1.6 broadcast_in_dim.4
  118.7 9.3 %while.16 = (s32[]{:T(128)}, f32[512,1024]{1,0:T(8,128)}, s32[]{:T(128)}, bf16[16,256,512]{2,1,0:T(8,128)(2,1)}, bf16[256,1024]{1,0:T(8,128)(2,1)}, /*index=5*/b...) while((s32[]{:T(128)}, f32[512,1024]{1,0:T(8,128)}, ...), condition=%wide.region_3.4_spmd, body=%wide.region_0.3_spmd.sunk | while | flops 1345323008 | bytes 26214732 | solution.py:90
  118.7 9.0 %conditional.2 = (f32[512,1024]{1,0:T(8,128)}) conditional(s32[]{:T(128)} %convert_element_type.104, f32[512,1024]{1,0:T(8,128)} %get-tuple-element.261, (s32[]{:T(128)}, bf16[16,256,512]{2,1,0:T(8,128)(2,1)}, bf16[256,1024]{1,0:T(8,128)(2,1)}, bf16[256,1024]{1,0:T(8,128)(2,1)}, s32[]{:T(128)}, /*index=5*/f32[4096,512]{1,0:T(8,128)}, ...), branch_computations={%region_1.1_spmd, %region_2.2_spmd} | conditional | flops 1345323008 | bytes 26214540 | solution.py:88
  118.7 0.0 copy-start
  118.7 1.6 fusion.3
  120.3 0.0 copy-done
  120.3 1.4 convolution_add_fusion
  121.7 2.1 fusion
  123.8 0.5 multiply_subtract_fusion
  124.3 3.3 %maximum_add_fusion = f32[512,1024]{1,0:T(8,128)} fusion(f32[512,1024]{1,0:T(8,128)} %get-tuple-element.158, f32[512,512]{1,0:T(8,128)S(1)} %get-tuple-element.194, f32[512,512]{1,0:T(8,128)S(1)} %get-tuple-element.193), kind=kLoop, calls=%fused_computation | loop fusion | flops 1048576 | bytes 6291456 | tf_op jit(solution)/shard_map/while/body/eval_jaxpr/cond/branch_1_fun/add | solution.py:84
  128.0 0.0 copy-start.1
  128.0 0.0 copy-start.2
  128.0 0.0 copy-start.3
  128.0 5.9 %fusion.10 = f32[512,512]{1,0:T(8,128)S(1)} fusion(f32[512,1024]{1,0:T(8,128)} %get-tuple-element.176, f32[512,512]{1,0:T(8,128)} %get-tuple-element.199, f32[512,512]{1,0:T(8,128)} %get-tuple-element.200), kind=kOutput, calls=%fused_computation.16 | convolution fusion | flops 1611661312 | bytes 5242880 | tf_op jit(solution)/shard_map/dot_general | solution.py:91
  134.0 12.3 %collective-permute-start = (bf16[256,512]{1,0:T(8,128)(2,1)S(1)}, bf16[256,512]{1,0:T(8,128)(2,1)S(1)}, u32[]{:S(2)}, u32[]{:S(2)}) collective-permute-start(bf16[256,512]{1,0:T(8,128)(2,1)S(1)} %slice.44), channel_id=1, source_target_pairs={{0,8},{8,16},{16,24},{24,32},{32,40},{40,48},{48,56},{56,64},{64,7... | collective-permute-start | bytes 786440 | tf_op jit(solution)/shard_map/ppermute | solution.py:11
  146.3 32.7 %all-gather.7.cloned.1.call-done = bf16[512,4096]{1,0:T(8,128)(2,1)} async-done(((bf16[512,256]{1,0:T(8,128)(2,1)}), bf16[512,4096]{1,0:T(8,128)(2,1)}) %all-gather.7.cloned.1.call-update) | async-done | bytes 4194320 | tf_op jit(solution)/shard_map/all_gather | solution.py:104
  179.0 0.0 collective-permute-done
  179.0 0.0 copy-done.1
  179.0 0.0 copy-done.2
  179.0 0.0 copy-done.3
  179.0 4.8 %convolution_convert_fusion = bf16[256,4096]{1,0:T(8,128)(2,1)} fusion(bf16[512,4096]{1,0:T(8,128)(2,1)} %all-gather.7.cloned.1.call-done, f32[512,512]{1,0:T(8,128)S(1)} %fusion.10, bf16[256,512]{1,0:T(8,128)(2,1)S(1)} %copy-done.1, bf16[256,512]{1,0:T(8,128)(2,1)S(1)} %collective-permute-done, bf16[256,512]{1,0:T(8,128)(2,1)S(1)} %copy-done.2, ...), kind=kOutput, calls=%fused_computation.14 | convolution fusion | flops 1075838976 | bytes 7604224 | tf_op jit(solution)/shard_map/dot_general | solution.py:103
  183.8 0.0 reduce-scatter.2.cloned.1.call-update
  183.8 132.1 %reduce-scatter.2.cloned.1.call-done = bf16[256,512]{1,0:T(8,128)(2,1)} async-done(((bf16[256,4096]{1,0:T(8,128)(2,1)}), bf16[256,512]{1,0:T(8,128)(2,1)}) %reduce-scatter.2.cloned.1.call-update) | async-done | bytes 262160 | tf_op jit(solution)/shard_map/reduce_scatter | solution.py:106
  (16 shorter events, 0.1 us)
Async XLA Ops:
  6.5 57.1 %all-gather.5.cloned.1.call-start = ((), (), s32[]{:S(2)}) async-start(), calls=%async_computation.1 | async-start | bytes 4456448 | tf_op jit(solution)/shard_map/all_gather | solution.py:69
  8.3 108.7 %all-gather.9.cloned.1.call-start = ((), (), s32[]{:S(2)}) async-start(), calls=%async_computation.4 | async-start | bytes 4456448 | tf_op jit(solution)/shard_map/all_gather | solution.py:74
  10.2 168.8 %all-gather.7.cloned.1.call-start = ((), (), s32[]{:S(2)}) async-start(), calls=%async_computation.2 | async-start | bytes 4456448 | tf_op jit(solution)/shard_map/all_gather | solution.py:104
  10.9 304.9 %reduce-scatter.2.cloned.1.call-start = ((), (), s32[]{:S(2)}) async-start(), calls=%async_computation.3 | async-start | bytes 2359296 | tf_op jit(solution)/shard_map/reduce_scatter | solution.py:106
  118.7 1.6 copy-start
  128.0 51.0 %copy-start.1 = (bf16[256,512]{1,0:T(8,128)(2,1)S(1)}, bf16[256,512]{1,0:T(8,128)(2,1)}, u32[]{:S(2)}) copy-start(bf16[256,512]{1,0:T(8,128)(2,1)} %multiply_convert_fusion) | copy-start | bytes 786436
  128.0 51.0 %copy-start.2 = (bf16[256,512]{1,0:T(8,128)(2,1)S(1)}, bf16[256,512]{1,0:T(8,128)(2,1)}, u32[]{:S(2)}) copy-start(bf16[256,512]{1,0:T(8,128)(2,1)} %param.10) | copy-start | bytes 786436
  128.0 51.0 %copy-start.3 = (f32[512]{0:T(512)S(1)}, f32[512]{0:T(512)}, u32[]{:S(2)}) copy-start(f32[512]{0:T(512)} %param.14) | copy-start | bytes 6148
  134.0 45.0 %collective-permute-start = (bf16[256,512]{1,0:T(8,128)(2,1)S(1)}, bf16[256,512]{1,0:T(8,128)(2,1)S(1)}, u32[]{:S(2)}, u32[]{:S(2)}) collective-permute-start(bf16[256,512]{1,0:T(8,128)(2,1)S(1)} %slice.44), channel_id=1, source_target_pairs={{0,8},{8,16},{16,24},{24,32},{32,40},{40,48},{48,56},{56,64},{64,7... | collective-permute-start | bytes 786440 | tf_op jit(solution)/shard_map/ppermute | solution.py:11
Sparse Core Ops, SparseCore 0:
  9.5 54.1 all-gather.4
  65.8 51.2 all-gather.8
  119.2 59.7 all-gather.6
  183.9 131.8 reduce-scatter.1
where the time goes:
time: 325 us; the launch traced here: 322 us
  waiting for transfers between devices  256 us (79%)
  other arithmetic  22.9 us (7%)
  matrix products  15.8 us (5%)
  between operations  13.2 us (4%)
  starting transfers between devices  12.5 us (4%)
    reduce_scatter x1, waiting for transfers between devices, per_device(): lax.psum_scatter(partial_rows.astype(jnp.bfloat16), 'ch', scatter_dimensi...  132 us
    all_gather x1, waiting for transfers between devices, per_device(): piece = lax.all_gather(gated[None], 'ctx', axis=0, tiled=True)  46.8 us
    all_gather x1, waiting for transfers between devices, per_device(): lax.all_gather(filters.astype(jnp.bfloat16), 'ctx', axis=0, tiled=True)  43.8 us
    all_gather x1, waiting for transfers between devices, per_device(): lax.all_gather(w_out, 'ctx', axis=1, tiled=True)  32.7 us
    ppermute x1, starting transfers between devices, from_behind(): return lax.ppermute(block, axis, route)  12.3 us
    convert_element_type x1, other arithmetic, per_device(): lax.all_gather(filters.astype(jnp.bfloat16), 'ctx', axis=0, tiled=True)  6.63 us
  transfers between devices with their start and end apart: 5, of which 4 were waited for; matrix products, arithmetic and copies ran while one was open for 10% of the time, Pallas kernels for 0%

commit v1 on v0

--- a/solution.py
+++ b/solution.py
@@ -3,6 +3,7 @@
 import jax.numpy as jnp
 from jax import lax
 from jax.sharding import PartitionSpec as P
+from jax.lax import axis_index, ppermute, psum
 
 
 def from_behind(block, axis, distance):
@@ -59,6 +60,25 @@
 
 
 def per_device(outer_gate, inner_gate, values_in, filters, skip_gain, w_out):
+
+    def _touch_regions(shard_in):
+        p_count = psum(1, axis_name="ctx")
+        stack_in = []
+        for it in tuple(range(p_count)):
+            stack_in.append((it, (it + 1) % p_count))
+        pile = []
+        for it in tuple(range(p_count)):
+            pile.append((it, (it - 1) % p_count))
+        left_arr, frame_out = ([shard_in], [shard_in])
+        for _ in range(p_count // 2):
+            passed = ppermute(left_arr[-1], axis_name="ctx", perm=stack_in)
+            left_arr.append(passed)
+        for _ in [*range((p_count - 1) // 2)]:
+            all_rows = ppermute(frame_out[-1], axis_name="ctx", perm=pile)
+            frame_out.append(all_rows)
+        current_arr = jnp.concatenate([*left_arr[::-1], *frame_out[1:]], 1)
+        return jnp.roll(current_arr, (axis_index("ctx") - p_count // 2) * shard_in.shape[1], axis=1)
+
     block = outer_gate.shape[0]
     chans = outer_gate.shape[1]
     length = 2 * block
@@ -100,9 +120,7 @@
     mix_in = (
         outer_gate.astype(jnp.float32) * (conv + skip_gain[None, :] * gated.astype(jnp.float32))
     ).astype(jnp.bfloat16)
-    partial_rows = jnp.dot(
-        mix_in, lax.all_gather(w_out, "ctx", axis=1, tiled=True), preferred_element_type=jnp.float32
-    )
+    partial_rows = jnp.dot(mix_in, _touch_regions(w_out), preferred_element_type=jnp.float32)
     return lax.psum_scatter(
         partial_rows.astype(jnp.bfloat16), "ch", scatter_dimension=1, tiled=True
     )

time: 325 us -> 307 us (0.945)
  waiting for transfers between devices: 256 us -> 181 us
  starting transfers between devices: 12.5 us -> 45.4 us
  local copies, waits for them, and re-layouts: 1.64 us -> 29.8 us
    ppermute x0 -> x15, waiting for transfers between devices: none -> 55.3 us  [the longest x8 49.8 us: _touch_regions(): passed = ppermute(left_arr[-1], axis_name='ctx', perm=stack_in)]
    all_gather x1, waiting for transfers between devices: 46.8 us -> 0.01 us  [per_device(): piece = lax.all_gather(gated[None], 'ctx', axis=0, tiled=True)]
    all_gather x1, waiting for transfers between devices: 43.8 us -> 0.01 us  [per_device(): lax.all_gather(filters.astype(jnp.bfloat16), 'ctx', axis=0, tiled=True)]
    ppermute x0 -> x15, starting transfers between devices: none -> 40.3 us  [the longest x7 38.6 us: _touch_regions(): all_rows = ppermute(frame_out[-1], axis_name='ctx', perm=pile)]
    all_gather x1 -> x0, waiting for transfers between devices: 32.7 us -> none  [per_device(): lax.all_gather(w_out, 'ctx', axis=1, tiled=True)]
    unnamed x6 -> x47, local copies, waits for them, and re-layouts: 0.02 us -> 27.9 us
    ppermute x1, starting transfers between devices: 12.3 us -> 4.96 us  [from_behind(): return lax.ppermute(block, axis, route)]
    reduce_scatter x1, waiting for transfers between devices: 132 us -> 125 us  [per_device(): lax.psum_scatter(partial_rows.astype(jnp.bfloat16), 'ch', scatter_dimensi...]
  transfers between devices with their start and end apart: 5 -> 19, of which waited for: 4 -> 10; matrix products, arithmetic and copies ran while one was open for 10% -> 15% of each run, Pallas kernels for 0% -> 0%
where the time goes in v1:
time: 307 us; the launch traced here: 305 us
  waiting for transfers between devices  181 us (59%)
  starting transfers between devices  45.4 us (15%)
  local copies, waits for them, and re-layouts  29.8 us (10%)
  other arithmetic  20.2 us (7%)
  matrix products  15.2 us (5%)
  between operations  13.2 us (4%)
    reduce_scatter x1, waiting for transfers between devices, per_device(): lax.psum_scatter(partial_rows.astype(jnp.bfloat16), 'ch', scatter_dimensi...  125 us
    ppermute x8, waiting for transfers between devices, _touch_regions(): passed = ppermute(left_arr[-1], axis_name='ctx', perm=stack_in)  49.8 us
    ppermute x7, starting transfers between devices, _touch_regions(): all_rows = ppermute(frame_out[-1], axis_name='ctx', perm=pile)  38.6 us
    unnamed x47, local copies, waits for them, and re-layouts  27.9 us
    convert_element_type x1, other arithmetic, per_device(): lax.all_gather(filters.astype(jnp.bfloat16), 'ctx', axis=0, tiled=True)  6.66 us
  transfers between devices with their start and end apart: 19, of which 10 were waited for; matrix products, arithmetic and copies ran while one was open for 15% of the time, Pallas kernels for 0%

profile of v1, /device:TPU:0, one launch (start us, length us, event | category | flops | bytes accessed | tf_op | source)
XLA Modules:
  0.0 305.2 jit_solution(7096015996779961958)
XLA Ops:
  6.5 1.8 convert_element_type.66
  8.4 1.8 multiply_convert_fusion
  10.3 1.7 collective-permute-start.1
  12.0 11.4 %collective-permute-done.1 = bf16[512,256]{1,0:T(8,128)(2,1)S(1)} collective-permute-done((bf16[512,256]{1,0:T(8,128)(2,1)}, bf16[512,256]{1,0:T(8,128)(2,1)S(1)}, u32[]{:S(2)}, u32[]{:S(2)}) %collective-permute-start.1) | collective-permute-done | bytes 262176 | tf_op jit(solution)/shard_map/ppermute | solution.py:74
  23.4 5.3 %collective-permute-start.9 = (bf16[512,256]{1,0:T(8,128)(2,1)}, bf16[512,256]{1,0:T(8,128)(2,1)S(1)}, u32[]{:S(2)}, u32[]{:S(2)}) collective-permute-start(bf16[512,256]{1,0:T(8,128)(2,1)} %param.15), channel_id=1, source_target_pairs={{0,120},{8,0},{16,8},{24,16},{32,24},{40,32},{48,40},{56,48},{64,5... | collective-permute-start | bytes 786440 | tf_op jit(solution)/shard_map/ppermute | solution.py:77
  28.8 9.2 %collective-permute-done.2 = bf16[512,256]{1,0:T(8,128)(2,1)S(1)} collective-permute-done((bf16[512,256]{1,0:T(8,128)(2,1)S(1)}, bf16[512,256]{1,0:T(8,128)(2,1)S(1)}, u32[]{:S(2)}, u32[]{:S(2)}) %collective-permute-start.2) | collective-permute-done | bytes 262176 | tf_op jit(solution)/shard_map/ppermute | solution.py:74
  38.0 5.3 %collective-permute-start.10 = (bf16[512,256]{1,0:T(8,128)(2,1)S(1)}, bf16[512,256]{1,0:T(8,128)(2,1)S(1)}, u32[]{:S(2)}, u32[]{:S(2)}) collective-permute-start(bf16[512,256]{1,0:T(8,128)(2,1)S(1)} %collective-permute-done.9), channel_id=1, source_target_pairs={{0,120},{8,0},{16,8},{24,16},{32,24},{40,32},{48,40},{56,48},{64,5... | collective-permute-start | bytes 786440 | tf_op jit(solution)/shard_map/ppermute | solution.py:77
  43.4 5.4 %collective-permute-done.3 = bf16[512,256]{1,0:T(8,128)(2,1)S(1)} collective-permute-done((bf16[512,256]{1,0:T(8,128)(2,1)S(1)}, bf16[512,256]{1,0:T(8,128)(2,1)S(1)}, u32[]{:S(2)}, u32[]{:S(2)}) %collective-permute-start.3) | collective-permute-done | bytes 262176 | tf_op jit(solution)/shard_map/ppermute | solution.py:74
  48.7 3.3 %collective-permute-done.10 = bf16[512,256]{1,0:T(8,128)(2,1)S(1)} collective-permute-done((bf16[512,256]{1,0:T(8,128)(2,1)S(1)}, bf16[512,256]{1,0:T(8,128)(2,1)S(1)}, u32[]{:S(2)}, u32[]{:S(2)}) %collective-permute-start.10) | collective-permute-done | bytes 262176 | tf_op jit(solution)/shard_map/ppermute | solution.py:77
  52.1 5.8 %collective-permute-start.11 = (bf16[512,256]{1,0:T(8,128)(2,1)S(1)}, bf16[512,256]{1,0:T(8,128)(2,1)S(1)}, u32[]{:S(2)}, u32[]{:S(2)}) collective-permute-start(bf16[512,256]{1,0:T(8,128)(2,1)S(1)} %collective-permute-done.10), channel_id=1, source_target_pairs={{0,120},{8,0},{16,8},{24,16},{32,24},{40,32},{48,40},{56,48},{64,5... | collective-permute-start | bytes 786440 | tf_op jit(solution)/shard_map/ppermute | solution.py:77
  57.9 8.0 %collective-permute-done.4 = bf16[512,256]{1,0:T(8,128)(2,1)S(1)} collective-permute-done((bf16[512,256]{1,0:T(8,128)(2,1)S(1)}, bf16[512,256]{1,0:T(8,128)(2,1)S(1)}, u32[]{:S(2)}, u32[]{:S(2)}) %collective-permute-start.4) | collective-permute-done | bytes 262176 | tf_op jit(solution)/shard_map/ppermute | solution.py:74
  65.9 2.1 collective-permute-done.11
  67.9 5.8 %collective-permute-start.12 = (bf16[512,256]{1,0:T(8,128)(2,1)S(1)}, bf16[512,256]{1,0:T(8,128)(2,1)S(1)}, u32[]{:S(2)}, u32[]{:S(2)}) collective-permute-start(bf16[512,256]{1,0:T(8,128)(2,1)S(1)} %collective-permute-done.11), channel_id=1, source_target_pairs={{0,120},{8,0},{16,8},{24,16},{32,24},{40,32},{48,40},{56,48},{64,5... | collective-permute-start | bytes 786440 | tf_op jit(solution)/shard_map/ppermute | solution.py:77
  73.7 6.1 %collective-permute-done.5 = bf16[512,256]{1,0:T(8,128)(2,1)S(1)} collective-permute-done((bf16[512,256]{1,0:T(8,128)(2,1)S(1)}, bf16[512,256]{1,0:T(8,128)(2,1)S(1)}, u32[]{:S(2)}, u32[]{:S(2)}) %collective-permute-start.5) | collective-permute-done | bytes 262176 | tf_op jit(solution)/shard_map/ppermute | solution.py:74
  79.8 5.3 %collective-permute-start.13 = (bf16[512,256]{1,0:T(8,128)(2,1)S(1)}, bf16[512,256]{1,0:T(8,128)(2,1)S(1)}, u32[]{:S(2)}, u32[]{:S(2)}) collective-permute-start(bf16[512,256]{1,0:T(8,128)(2,1)S(1)} %collective-permute-done.12), channel_id=1, source_target_pairs={{0,120},{8,0},{16,8},{24,16},{32,24},{40,32},{48,40},{56,48},{64,5... | collective-permute-start | bytes 786440 | tf_op jit(solution)/shard_map/ppermute | solution.py:77
  85.1 5.1 %collective-permute-done.6 = bf16[512,256]{1,0:T(8,128)(2,1)} collective-permute-done((bf16[512,256]{1,0:T(8,128)(2,1)S(1)}, bf16[512,256]{1,0:T(8,128)(2,1)}, u32[]{:S(2)}, u32[]{:S(2)}) %collective-permute-start.6) | collective-permute-done | bytes 262176 | tf_op jit(solution)/shard_map/ppermute | solution.py:74
  90.3 2.1 sine_negate_fusion.1
  92.4 1.0 pad_maximum_fusion
  93.3 5.3 %collective-permute-start.14 = (bf16[512,256]{1,0:T(8,128)(2,1)S(1)}, bf16[512,256]{1,0:T(8,128)(2,1)S(1)}, u32[]{:S(2)}, u32[]{:S(2)}) collective-permute-start(bf16[512,256]{1,0:T(8,128)(2,1)S(1)} %collective-permute-done.13), channel_id=1, source_target_pairs={{0,120},{8,0},{16,8},{24,16},{32,24},{40,32},{48,40},{56,48},{64,5... | collective-permute-start | bytes 786440 | tf_op jit(solution)/shard_map/ppermute | solution.py:77
  98.7 4.7 %collective-permute-done.7 = bf16[512,256]{1,0:T(8,128)(2,1)S(1)} collective-permute-done((bf16[512,256]{1,0:T(8,128)(2,1)}, bf16[512,256]{1,0:T(8,128)(2,1)S(1)}, u32[]{:S(2)}, u32[]{:S(2)}) %collective-permute-start.7) | collective-permute-done | bytes 262176 | tf_op jit(solution)/shard_map/ppermute | solution.py:74
  103.3 0.8 fusion.37
  104.2 5.0 %sine_negate_fusion = (f32[512,512]{1,0:T(8,128)}, f32[512,512]{1,0:T(8,128)}) fusion(), kind=kLoop, calls=%fused_computation.29 | loop fusion | flops 3932160 | bytes 2097152 | tf_op jit(solution)/shard_map/neg | solution.py:28
  109.2 5.6 %collective-permute-start.15 = (bf16[512,256]{1,0:T(8,128)(2,1)S(1)}, bf16[512,256]{1,0:T(8,128)(2,1)S(1)}, u32[]{:S(2)}, u32[]{:S(2)}) collective-permute-start(bf16[512,256]{1,0:T(8,128)(2,1)S(1)} %collective-permute-done.14), channel_id=1, source_target_pairs={{0,120},{8,0},{16,8},{24,16},{32,24},{40,32},{48,40},{56,48},{64,5... | collective-permute-start | bytes 786440 | tf_op jit(solution)/shard_map/ppermute | solution.py:77
  116.2 1.7 constant_dynamic-update-slice_fusion.29
  118.0 1.7 constant_dynamic-update-slice_fusion.28
  123.3 0.8 constant_dynamic-update-slice_fusion.22
  124.1 0.8 constant_dynamic-update-slice_fusion.21
  125.6 0.8 constant_dynamic-update-slice_fusion.19
  126.4 0.8 constant_dynamic-update-slice_fusion.18
  127.9 0.8 constant_dynamic-update-slice_fusion.16
  130.2 1.7 constant_dynamic-update-slice_fusion.13
  131.8 0.8 constant_dynamic-update-slice_fusion.12
  134.8 0.8 constant_dynamic-update-slice_fusion.8
  136.3 0.8 constant_dynamic-update-slice_fusion.6
  138.6 0.7 constant_dynamic-update-slice_fusion.3
  139.3 6.7 %convert_element_type.67 = f32[4096,512]{1,0:T(8,128)} convert(bf16[4096,512]{1,0:T(8,128)(2,1)} %all-gather.4.cloned.1.call-done) | non-fusion elementwise | flops 2097152 | bytes 12582912 | tf_op jit(solution)/shard_map/convert_element_type | solution.py:89
  146.2 7.0 %while.16 = (s32[]{:T(128)}, f32[512,1024]{1,0:T(8,128)S(1)}, s32[]{:T(128)}, bf16[16,256,512]{2,1,0:T(8,128)(2,1)}, bf16[256,1024]{1,0:T(8,128)(2,1)}, /*index=...) while((s32[]{:T(128)}, f32[512,1024]{1,0:T(8,128)S(1)}, ...), condition=%wide.region_3.4_spmd, body=%wide.region_0.3_spmd.sunk | while | flops 1345323008 | bytes 24117560 | solution.py:110
  146.3 6.4 %conditional.2 = (f32[512,1024]{1,0:T(8,128)S(1)}) conditional(s32[]{:T(128)} %convert_element_type.104, f32[512,1024]{1,0:T(8,128)S(1)} %get-tuple-element.261, (s32[]{:T(128)}, bf16[16,256,512]{2,1,0:T(8,128)(2,1)}, bf16[256,1024]{1,0:T(8,128)(2,1)}, bf16[256,1024]{1,0:T(8,128)(2,1)}, s32[]{:T(128)}, /*index=5*/f32[4096,512]{1,0:T(8,128)}, ...), branch_computations={%region_1.1_spmd, %region_2.2_spmd} | conditional | flops 1345323008 | bytes 24117360 | solution.py:108
  146.3 2.1 fusion
  148.4 1.6 fusion.3
  150.0 1.6 convolution_add_fusion
  153.3 5.0 %fusion.11 = f32[512,512]{1,0:T(8,128)S(1)} fusion(f32[512,1024]{1,0:T(8,128)S(1)} %get-tuple-element.176, f32[512,512]{1,0:T(8,128)} %get-tuple-element.199, f32[512,512]{1,0:T(8,128)} %get-tuple-element.200), kind=kOutput, calls=%fused_computation.17 | convolution fusion | flops 1611661312 | bytes 5242880 | tf_op jit(solution)/shard_map/dot_general | solution.py:111
  158.4 5.0 %collective-permute-start = (bf16[256,512]{1,0:T(8,128)(2,1)S(1)}, bf16[256,512]{1,0:T(8,128)(2,1)S(1)}, u32[]{:S(2)}, u32[]{:S(2)}) collective-permute-start(bf16[256,512]{1,0:T(8,128)(2,1)S(1)} %slice.44), channel_id=1, source_target_pairs={{0,8},{8,16},{16,24},{24,32},{32,40},{40,48},{48,56},{56,64},{64,7... | collective-permute-start | bytes 786440 | tf_op jit(solution)/shard_map/ppermute | solution.py:12
  163.3 1.7 constant_dynamic-update-slice_fusion.2
  165.0 1.7 constant_dynamic-update-slice_fusion.1
  166.7 1.7 constant_dynamic-update-slice_fusion
  168.4 4.9 %convolution_convert_fusion = bf16[256,4096]{1,0:T(8,128)(2,1)} fusion(bf16[512,8192]{1,0:T(8,128)(2,1)} %constant_dynamic-update-slice_fusion, s32[]{:T(128)S(6)} %select_n.39, f32[512,512]{1,0:T(8,128)S(1)} %fusion.11, bf16[256,512]{1,0:T(8,128)(2,1)S(1)} %copy-done, bf16[256,512]{1,0:T(8,128)(2,1)S(1)} %collective-permute-done, ...), kind=kOutput, calls=%fused_computation.14 | convolution fusion | flops 1075838976 | bytes 7604228 | tf_op jit(solution)/shard_map/dot_general | solution.py:123
  173.3 125.4 %reduce-scatter.2.cloned.1.call-done = bf16[256,512]{1,0:T(8,128)(2,1)} async-done(((bf16[256,4096]{1,0:T(8,128)(2,1)}), bf16[256,512]{1,0:T(8,128)(2,1)}) %reduce-scatter.2.cloned.1.call-update) | async-done | bytes 262160 | tf_op jit(solution)/shard_map/reduce_scatter | solution.py:124
  (74 shorter events, 14.1 us)
Async XLA Ops:
  6.5 116.0 %copy-start.1 = (bf16[512,256]{1,0:T(8,128)(2,1)S(1)}, bf16[512,256]{1,0:T(8,128)(2,1)}, u32[]{:S(2)}) copy-start(bf16[512,256]{1,0:T(8,128)(2,1)} %param.15) | copy-start | bytes 786436
  6.5 132.8 %all-gather.4.cloned.1.call-start = ((), (), s32[]{:S(2)}) async-start(), calls=%async_computation.1 | async-start | bytes 4456448 | tf_op jit(solution)/shard_map/all_gather | solution.py:89
  8.4 137.6 %all-gather.6.cloned.1.call-start = ((), (), s32[]{:S(2)}) async-start(), calls=%async_computation.3 | async-start | bytes 4456448 | tf_op jit(solution)/shard_map/all_gather | solution.py:94
  10.2 288.5 %reduce-scatter.2.cloned.1.call-start = ((), (), s32[]{:S(2)}) async-start(), calls=%async_computation.2 | async-start | bytes 2359296 | tf_op jit(solution)/shard_map/reduce_scatter | solution.py:124
  10.3 13.2 %collective-permute-start.1 = (bf16[512,256]{1,0:T(8,128)(2,1)}, bf16[512,256]{1,0:T(8,128)(2,1)S(1)}, u32[]{:S(2)}, u32[]{:S(2)}) collective-permute-start(bf16[512,256]{1,0:T(8,128)(2,1)} %param.15), channel_id=1, source_target_pairs={{0,8},{8,16},{16,24},{24,32},{32,40},{40,48},{48,56},{56,64},{64,7... | collective-permute-start | bytes 786440 | tf_op jit(solution)/shard_map/ppermute | solution.py:74
  23.4 14.6 %collective-permute-start.2 = (bf16[512,256]{1,0:T(8,128)(2,1)S(1)}, bf16[512,256]{1,0:T(8,128)(2,1)S(1)}, u32[]{:S(2)}, u32[]{:S(2)}) collective-permute-start(bf16[512,256]{1,0:T(8,128)(2,1)S(1)} %collective-permute-done.1), channel_id=1, source_target_pairs={{0,8},{8,16},{16,24},{24,32},{32,40},{40,48},{48,56},{56,64},{64,7... | collective-permute-start | bytes 786440 | tf_op jit(solution)/shard_map/ppermute | solution.py:74
  23.4 14.6 %collective-permute-start.9 = (bf16[512,256]{1,0:T(8,128)(2,1)}, bf16[512,256]{1,0:T(8,128)(2,1)S(1)}, u32[]{:S(2)}, u32[]{:S(2)}) collective-permute-start(bf16[512,256]{1,0:T(8,128)(2,1)} %param.15), channel_id=1, source_target_pairs={{0,120},{8,0},{16,8},{24,16},{32,24},{40,32},{48,40},{56,48},{64,5... | collective-permute-start | bytes 786440 | tf_op jit(solution)/shard_map/ppermute | solution.py:77
  38.0 10.7 %collective-permute-start.3 = (bf16[512,256]{1,0:T(8,128)(2,1)S(1)}, bf16[512,256]{1,0:T(8,128)(2,1)S(1)}, u32[]{:S(2)}, u32[]{:S(2)}) collective-permute-start(bf16[512,256]{1,0:T(8,128)(2,1)S(1)} %collective-permute-done.2), channel_id=1, source_target_pairs={{0,8},{8,16},{16,24},{24,32},{32,40},{40,48},{48,56},{56,64},{64,7... | collective-permute-start | bytes 786440 | tf_op jit(solution)/shard_map/ppermute | solution.py:74
  38.0 14.1 %collective-permute-start.10 = (bf16[512,256]{1,0:T(8,128)(2,1)S(1)}, bf16[512,256]{1,0:T(8,128)(2,1)S(1)}, u32[]{:S(2)}, u32[]{:S(2)}) collective-permute-start(bf16[512,256]{1,0:T(8,128)(2,1)S(1)} %collective-permute-done.9), channel_id=1, source_target_pairs={{0,120},{8,0},{16,8},{24,16},{32,24},{40,32},{48,40},{56,48},{64,5... | collective-permute-start | bytes 786440 | tf_op jit(solution)/shard_map/ppermute | solution.py:77
  48.7 17.1 %collective-permute-start.4 = (bf16[512,256]{1,0:T(8,128)(2,1)S(1)}, bf16[512,256]{1,0:T(8,128)(2,1)S(1)}, u32[]{:S(2)}, u32[]{:S(2)}) collective-permute-start(bf16[512,256]{1,0:T(8,128)(2,1)S(1)} %collective-permute-done.3), channel_id=1, source_target_pairs={{0,8},{8,16},{16,24},{24,32},{32,40},{40,48},{48,56},{56,64},{64,7... | collective-permute-start | bytes 786440 | tf_op jit(solution)/shard_map/ppermute | solution.py:74
  52.1 15.8 %collective-permute-start.11 = (bf16[512,256]{1,0:T(8,128)(2,1)S(1)}, bf16[512,256]{1,0:T(8,128)(2,1)S(1)}, u32[]{:S(2)}, u32[]{:S(2)}) collective-permute-start(bf16[512,256]{1,0:T(8,128)(2,1)S(1)} %collective-permute-done.10), channel_id=1, source_target_pairs={{0,120},{8,0},{16,8},{24,16},{32,24},{40,32},{48,40},{56,48},{64,5... | collective-permute-start | bytes 786440 | tf_op jit(solution)/shard_map/ppermute | solution.py:77
  65.8 13.9 %collective-permute-start.5 = (bf16[512,256]{1,0:T(8,128)(2,1)S(1)}, bf16[512,256]{1,0:T(8,128)(2,1)S(1)}, u32[]{:S(2)}, u32[]{:S(2)}) collective-permute-start(bf16[512,256]{1,0:T(8,128)(2,1)S(1)} %collective-permute-done.4), channel_id=1, source_target_pairs={{0,8},{8,16},{16,24},{24,32},{32,40},{40,48},{48,56},{56,64},{64,7... | collective-permute-start | bytes 786440 | tf_op jit(solution)/shard_map/ppermute | solution.py:74
  67.9 11.9 %collective-permute-start.12 = (bf16[512,256]{1,0:T(8,128)(2,1)S(1)}, bf16[512,256]{1,0:T(8,128)(2,1)S(1)}, u32[]{:S(2)}, u32[]{:S(2)}) collective-permute-start(bf16[512,256]{1,0:T(8,128)(2,1)S(1)} %collective-permute-done.11), channel_id=1, source_target_pairs={{0,120},{8,0},{16,8},{24,16},{32,24},{40,32},{48,40},{56,48},{64,5... | collective-permute-start | bytes 786440 | tf_op jit(solution)/shard_map/ppermute | solution.py:77
  79.8 12.6 %copy-start.5 = (bf16[512,256]{1,0:T(8,128)(2,1)}, bf16[512,256]{1,0:T(8,128)(2,1)S(1)}, u32[]{:S(2)}) copy-start(bf16[512,256]{1,0:T(8,128)(2,1)S(1)} %collective-permute-done.5) | copy-start | bytes 786436
  79.8 10.5 %collective-permute-start.6 = (bf16[512,256]{1,0:T(8,128)(2,1)S(1)}, bf16[512,256]{1,0:T(8,128)(2,1)}, u32[]{:S(2)}, u32[]{:S(2)}) collective-permute-start(bf16[512,256]{1,0:T(8,128)(2,1)S(1)} %collective-permute-done.5), channel_id=1, source_target_pairs={{0,8},{8,16},{16,24},{24,32},{32,40},{40,48},{48,56},{56,64},{64,7... | collective-permute-start | bytes 786440 | tf_op jit(solution)/shard_map/ppermute | solution.py:74
  79.8 13.6 %collective-permute-start.13 = (bf16[512,256]{1,0:T(8,128)(2,1)S(1)}, bf16[512,256]{1,0:T(8,128)(2,1)S(1)}, u32[]{:S(2)}, u32[]{:S(2)}) collective-permute-start(bf16[512,256]{1,0:T(8,128)(2,1)S(1)} %collective-permute-done.12), channel_id=1, source_target_pairs={{0,120},{8,0},{16,8},{24,16},{32,24},{40,32},{48,40},{56,48},{64,5... | collective-permute-start | bytes 786440 | tf_op jit(solution)/shard_map/ppermute | solution.py:77
  90.3 13.1 %collective-permute-start.7 = (bf16[512,256]{1,0:T(8,128)(2,1)}, bf16[512,256]{1,0:T(8,128)(2,1)S(1)}, u32[]{:S(2)}, u32[]{:S(2)}) collective-permute-start(bf16[512,256]{1,0:T(8,128)(2,1)} %collective-permute-done.6), channel_id=1, source_target_pairs={{0,8},{8,16},{16,24},{24,32},{32,40},{40,48},{48,56},{56,64},{64,7... | collective-permute-start | bytes 786440 | tf_op jit(solution)/shard_map/ppermute | solution.py:74
  92.4 39.5 %copy-start.6 = (bf16[512,256]{1,0:T(8,128)(2,1)S(1)}, bf16[512,256]{1,0:T(8,128)(2,1)}, u32[]{:S(2)}) copy-start(bf16[512,256]{1,0:T(8,128)(2,1)} %copy-done.5) | copy-start | bytes 786436
  93.3 43.0 %copy-start.2 = (bf16[512,256]{1,0:T(8,128)(2,1)}, bf16[512,256]{1,0:T(8,128)(2,1)S(1)}, u32[]{:S(2)}) copy-start(bf16[512,256]{1,0:T(8,128)(2,1)S(1)} %collective-permute-done.13) | copy-start | bytes 786436
  93.3 15.9 %collective-permute-start.14 = (bf16[512,256]{1,0:T(8,128)(2,1)S(1)}, bf16[512,256]{1,0:T(8,128)(2,1)S(1)}, u32[]{:S(2)}, u32[]{:S(2)}) collective-permute-start(bf16[512,256]{1,0:T(8,128)(2,1)S(1)} %collective-permute-done.13), channel_id=1, source_target_pairs={{0,120},{8,0},{16,8},{24,16},{32,24},{40,32},{48,40},{56,48},{64,5... | collective-permute-start | bytes 786440 | tf_op jit(solution)/shard_map/ppermute | solution.py:77
  103.3 11.4 %collective-permute-start.8 = (bf16[512,256]{1,0:T(8,128)(2,1)S(1)}, bf16[512,256]{1,0:T(8,128)(2,1)S(1)}, u32[]{:S(2)}, u32[]{:S(2)}) collective-permute-start(bf16[512,256]{1,0:T(8,128)(2,1)S(1)} %collective-permute-done.7), channel_id=1, source_target_pairs={{0,8},{8,16},{16,24},{24,32},{32,40},{40,48},{48,56},{56,64},{64,7... | collective-permute-start | bytes 786440 | tf_op jit(solution)/shard_map/ppermute | solution.py:74
  109.2 27.9 %copy-start.3 = (bf16[512,256]{1,0:T(8,128)(2,1)}, bf16[512,256]{1,0:T(8,128)(2,1)S(1)}, u32[]{:S(2)}) copy-start(bf16[512,256]{1,0:T(8,128)(2,1)S(1)} %collective-permute-done.14) | copy-start | bytes 786436
  109.2 18.7 %collective-permute-start.15 = (bf16[512,256]{1,0:T(8,128)(2,1)S(1)}, bf16[512,256]{1,0:T(8,128)(2,1)S(1)}, u32[]{:S(2)}, u32[]{:S(2)}) collective-permute-start(bf16[512,256]{1,0:T(8,128)(2,1)S(1)} %collective-permute-done.14), channel_id=1, source_target_pairs={{0,120},{8,0},{16,8},{24,16},{32,24},{40,32},{48,40},{56,48},{64,5... | collective-permute-start | bytes 786440 | tf_op jit(solution)/shard_map/ppermute | solution.py:77
  127.9 10.0 %copy-start.4 = (bf16[512,256]{1,0:T(8,128)(2,1)}, bf16[512,256]{1,0:T(8,128)(2,1)S(1)}, u32[]{:S(2)}) copy-start(bf16[512,256]{1,0:T(8,128)(2,1)S(1)} %collective-permute-done.15) | copy-start | bytes 786436
  146.2 22.2 %copy-start = (bf16[256,512]{1,0:T(8,128)(2,1)S(1)}, bf16[256,512]{1,0:T(8,128)(2,1)}, u32[]{:S(2)}) copy-start(bf16[256,512]{1,0:T(8,128)(2,1)} %multiply_convert_fusion) | copy-start | bytes 786436
  146.2 22.2 %copy-start.7 = (f32[512]{0:T(512)S(1)}, f32[512]{0:T(512)}, u32[]{:S(2)}) copy-start(f32[512]{0:T(512)} %param.14) | copy-start | bytes 6148
  158.4 10.0 %collective-permute-start = (bf16[256,512]{1,0:T(8,128)(2,1)S(1)}, bf16[256,512]{1,0:T(8,128)(2,1)S(1)}, u32[]{:S(2)}, u32[]{:S(2)}) collective-permute-start(bf16[256,512]{1,0:T(8,128)(2,1)S(1)} %slice.44), channel_id=1, source_target_pairs={{0,8},{8,16},{16,24},{24,32},{32,40},{40,48},{48,56},{56,64},{64,7... | collective-permute-start | bytes 786440 | tf_op jit(solution)/shard_map/ppermute | solution.py:12
Sparse Core Ops, SparseCore 0:
  9.5 67.4 all-gather.3
  79.1 55.6 all-gather.5
  173.5 125.1 reduce-scatter.1
